TPU v7x, 256 devices: a whole 4x4x8 slice. The times are simulated.
256 devices in a mesh: row: 16 (over x, y_lo, core), col: 16 (over y_hi, z).
Axes of the slice: x: 4, y: 4 (y_hi: 2, y_lo: 2; y = y_hi * 2 + y_lo), z: 8, core: 2. Of those that a mesh axis runs over, the one named last changes fastest.
Arguments:
- pair_state: bfloat16 [768, 768, 128], P('row', 'col'), may hold values from -6 to 6
- outgoing_norm: float32 [128], replicated, may hold values from 0.1 to 1.9
- outgoing_mixing: bfloat16 [128, 640], replicated, may hold values from -0.5 to 0.5
- outgoing_scale: float32 [128], replicated, may hold values from 0.1 to 1.9
- outgoing_final: bfloat16 [128, 128], replicated, may hold values from -0.5 to 0.5
- incoming_norm: float32 [128], replicated, may hold values from 0.1 to 1.9
- incoming_mixing: bfloat16 [128, 640], replicated, may hold values from -0.5 to 0.5
- incoming_scale: float32 [128], replicated, may hold values from 0.1 to 1.9
- incoming_final: bfloat16 [128, 128], replicated, may hold values from -0.5 to 0.5
Outputs:
- pair_out: bfloat16 [768, 768, 128], P('row', 'col')
All inputs are finite; a program needn't handle non-finite values.
Results may differ from a plain program's by a relative error of at most 0.018.
Values may be sent and summed in bfloat16 or wider, within the bound.
A program may use at most 128 MiB of HBM per device.

v0:
```python
import jax
import jax.numpy as jnp
from jax import lax
from jax.sharding import PartitionSpec as P


def normalize(values, channel_gain):
    floated = values.astype(jnp.float32)
    center = jnp.mean(floated, axis=-1, keepdims=True)
    spread = jnp.mean((floated - center) ** 2, axis=-1, keepdims=True)
    return ((floated - center) * lax.rsqrt(spread + 1e-05) * channel_gain).astype(jnp.bfloat16)


def gated_product(normed, weights, column):
    width = weights.shape[0]
    flat = normed.reshape(-1, width)
    gating = jnp.dot(
        flat, weights[:, column * width : (column + 1) * width], preferred_element_type=jnp.float32
    )
    content = jnp.dot(
        flat,
        weights[:, (column + 1) * width : (column + 2) * width],
        preferred_element_type=jnp.float32,
    )
    return (jax.nn.sigmoid(gating) * content).astype(jnp.bfloat16).reshape(normed.shape)


def finish_update(pair_field, normed, product, weights, scale, final):
    width = weights.shape[0]
    mixed = normalize(product, scale)
    gating = jax.nn.sigmoid(
        jnp.dot(
            normed.reshape(-1, width), weights[:, 4 * width :], preferred_element_type=jnp.float32
        )
    )
    update = gating * jnp.dot(mixed.reshape(-1, width), final, preferred_element_type=jnp.float32)
    return (pair_field.astype(jnp.float32) + update.reshape(pair_field.shape)).astype(jnp.bfloat16)


def body(
    pair_state,
    outgoing_norm,
    outgoing_mixing,
    outgoing_scale,
    outgoing_final,
    incoming_norm,
    incoming_mixing,
    incoming_scale,
    incoming_final,
):
    normed = normalize(pair_state, outgoing_norm)
    first_factor = gated_product(normed, outgoing_mixing, 0)
    second_factor = gated_product(normed, outgoing_mixing, 2)
    gathered = lax.all_gather(second_factor, "row", axis=0, tiled=True)
    sliced = gathered
    summed = lax.psum_scatter(
        jnp.einsum("jkc,ikc->jic", sliced, first_factor, preferred_element_type=jnp.float32).astype(
            jnp.bfloat16
        ),
        "col",
        scatter_dimension=0,
        tiled=True,
    ).astype(jnp.float32)
    product = jnp.transpose(summed, (1, 0, 2))
    middle = finish_update(
        pair_state, normed, product, outgoing_mixing, outgoing_scale, outgoing_final
    )
    normed_second = normalize(middle, incoming_norm)
    later_factor = gated_product(normed_second, incoming_mixing, 2)
    early_factor = gated_product(normed_second, incoming_mixing, 0)
    collected = lax.all_gather(early_factor, "col", axis=1, tiled=True)
    sliced = collected
    product_second = lax.psum_scatter(
        jnp.einsum("kic,kjc->ijc", sliced, later_factor, preferred_element_type=jnp.float32).astype(
            jnp.bfloat16
        ),
        "row",
        scatter_dimension=0,
        tiled=True,
    ).astype(jnp.float32)
    return finish_update(
        middle, normed_second, product_second, incoming_mixing, incoming_scale, incoming_final
    )


def solution(mesh):
    placed = (P("row", "col", None), P(), P(), P(), P(), P(), P(), P(), P())
    return jax.shard_map(
        body, mesh=mesh, in_specs=placed, out_specs=P("row", "col", None), check_vma=False
    )
```

profile of v0, /device:TPU:1, one launch (start us, length us, event | category | flops | bytes accessed | tf_op | source)
XLA Modules:
  0.0 725.3 jit_solution(701455853628976289)
XLA Ops:
  6.5 0.0 all-gather.3.cloned.1.call-start
  6.6 1.5 convert_reduce_fusion.1
  8.1 1.8 fusion.31
  9.9 0.8 fusion.33
  10.7 0.5 fusion.11
  11.2 0.3 fusion.19
  11.5 1.8 copy.42
  13.2 0.0 all-gather.3.cloned.1.call-update
  13.3 0.0 reduce-scatter.3.cloned.1.call-start
  13.3 0.5 fusion.14
  13.8 0.3 fusion.18
  14.1 1.0 copy.43
  15.0 136.2 %all-gather.3.cloned.1.call-done = bf16[768,48,128]{1,0,2:T(8,128)(2,1)} async-done(((bf16[48,48,128]{1,0,2:T(8,128)(2,1)}), bf16[768,48,128]{1,0,2:T(8,128)(2,1)}) %all-gather.3.cloned.1.call-update) | async-done | bytes 9437200 | tf_op jit(solution)/shard_map/all_gather | solution.py:54
  151.2 16.8 %convert_bitcast_fusion.1 = bf16[768,48,128]{0,1,2:T(8,128)(2,1)} fusion(bf16[48,48,128]{1,0,2:T(8,128)(2,1)S(1)} %copy.43, bf16[768,48,128]{1,0,2:T(8,128)(2,1)} %all-gather.3.cloned.1.call-done), kind=kOutput, calls=%fused_computation.1 | convolution fusion | flops 457703424 | bytes 19464192 | tf_op jit(solution)/shard_map/jkc,ikc->jic/dot_general | solution.py:57
  168.0 14.0 %copy.44 = bf16[768,48,128]{2,1,0:T(8,128)(2,1)} copy(bf16[768,48,128]{0,1,2:T(8,128)(2,1)} %convert_bitcast_fusion.1) | data formatting | bytes 18874368 | tf_op jit(solution)/shard_map/convert_element_type | solution.py:57
  182.0 0.0 reduce-scatter.3.cloned.1.call-update
  182.0 0.0 all-gather.5.cloned.1.call-start
  182.1 0.5 fusion.17
  182.6 230.1 %reduce-scatter.3.cloned.1.call-done = bf16[48,48,128]{2,1,0:T(8,128)(2,1)} async-done(((bf16[768,48,128]{2,1,0:T(8,128)(2,1)}), bf16[48,48,128]{2,1,0:T(8,128)(2,1)}) %reduce-scatter.3.cloned.1.call-update) | async-done | bytes 589840 | tf_op jit(solution)/shard_map/reduce_scatter | solution.py:56
  412.7 1.5 bitcast_reduce_fusion
  414.2 1.8 fusion.41
  416.0 0.9 fusion.43
  416.9 0.3 convolution_multiply_fusion.3
  417.2 0.0 copy-start.10
  417.2 0.4 convert_reduce_fusion
  417.6 0.7 fusion.28
  418.4 0.8 fusion.30
  419.2 0.5 fusion.2
  419.6 0.3 fusion.21
  419.9 1.0 copy.46
  420.9 0.0 all-gather.5.cloned.1.call-update
  420.9 0.2 reduce-scatter.5.cloned.1.call-start
  421.2 0.5 fusion.5
  421.6 0.3 fusion.20
  421.9 1.1 copy.47
  423.0 145.3 %all-gather.5.cloned.1.call-done = bf16[48,768,128]{2,0,1:T(8,128)(2,1)} async-done(((bf16[48,48,128]{2,0,1:T(8,128)(2,1)}), bf16[48,768,128]{2,0,1:T(8,128)(2,1)}) %all-gather.5.cloned.1.call-update) | async-done | bytes 9437200 | tf_op jit(solution)/shard_map/all_gather | solution.py:71
  568.3 14.0 %copy.48 = bf16[48,768,128]{1,0,2:T(8,128)(2,1)} copy(bf16[48,768,128]{2,0,1:T(8,128)(2,1)} %all-gather.5.cloned.1.call-done) | data formatting | bytes 18874368 | tf_op jit(solution)/shard_map/all_gather | solution.py:71
  582.4 9.9 %convert_bitcast_fusion = bf16[768,48,128]{0,1,2:T(8,128)(2,1)} fusion(bf16[48,48,128]{0,1,2:T(8,128)(2,1)S(1)} %copy.47, bf16[48,768,128]{1,0,2:T(8,128)(2,1)} %copy.48), kind=kOutput, calls=%fused_computation | convolution fusion | flops 457703424 | bytes 19464192 | tf_op jit(solution)/shard_map/kic,kjc->ijc/dot_general | solution.py:74
  592.3 14.0 %copy.49 = bf16[768,48,128]{2,1,0:T(8,128)(2,1)} copy(bf16[768,48,128]{0,1,2:T(8,128)(2,1)} %convert_bitcast_fusion) | data formatting | bytes 18874368 | tf_op jit(solution)/shard_map/convert_element_type | solution.py:74
  606.3 0.0 reduce-scatter.5.cloned.1.call-update
  606.3 0.5 fusion.8
  606.8 106.6 %reduce-scatter.5.cloned.1.call-done = bf16[48,48,128]{2,1,0:T(8,128)(2,1)} async-done(((bf16[768,48,128]{2,1,0:T(8,128)(2,1)}), bf16[48,48,128]{2,1,0:T(8,128)(2,1)}) %reduce-scatter.5.cloned.1.call-update) | async-done | bytes 589840 | tf_op jit(solution)/shard_map/reduce_scatter | solution.py:73
  713.4 1.5 convert_reduce_fusion.2
  714.9 1.8 fusion.34
  716.7 0.8 fusion.36
  717.5 0.3 convolution_multiply_fusion
  717.8 0.0 copy-start.1
  717.8 0.9 fusion.38
  (30 shorter events, 0.1 us)
Async XLA Ops:
  6.5 410.3 %copy-start = (bf16[128,128]{1,0:T(8,128)(2,1)S(1)}, bf16[128,128]{1,0:T(8,128)(2,1)}, u32[]{:S(2)}) copy-start(bf16[128,128]{1,0:T(8,128)(2,1)} %param.13) | copy-start | bytes 98308
  6.5 3.4 copy-start.2
  6.5 3.4 copy-start.8
  6.5 4.2 copy-start.6
  6.5 144.7 %all-gather.3.cloned.1.call-start = ((), (), s32[]{:S(2)}) async-start(), calls=%async_computation.2 | async-start | bytes 26738688 | tf_op jit(solution)/shard_map/all_gather | solution.py:54
  13.3 399.4 %reduce-scatter.3.cloned.1.call-start = ((), (), s32[]{:S(2)}) async-start(), calls=%async_computation.3 | async-start | bytes 10027008 | tf_op jit(solution)/shard_map/reduce_scatter | solution.py:56
  182.0 386.3 %all-gather.5.cloned.1.call-start = ((), (), s32[]{:S(2)}) async-start(), calls=%async_computation.4 | async-start | bytes 10027008 | tf_op jit(solution)/shard_map/all_gather | solution.py:71
  182.5 233.4 %copy-start.9 = (f32[128]{0:T(128)S(1)}, f32[128]{0:T(128)}, u32[]{:S(2)}) copy-start(f32[128]{0:T(128)} %param.12) | copy-start | bytes 1540
  412.7 3.3 copy-start.3
  417.2 1.2 copy-start.10
  417.6 1.5 copy-start.7
  420.9 292.4 %reduce-scatter.5.cloned.1.call-start = ((), (), s32[]{:S(2)}) async-start(), calls=%async_computation.5 | async-start | bytes 10027008 | tf_op jit(solution)/shard_map/reduce_scatter | solution.py:73
  606.8 109.9 %copy-start.11 = (f32[128]{0:T(128)S(1)}, f32[128]{0:T(128)}, u32[]{:S(2)}) copy-start(f32[128]{0:T(128)} %param.16) | copy-start | bytes 1540
  606.8 110.7 %copy-start.5 = (bf16[128,128]{1,0:T(8,128)(2,1)S(1)}, bf16[128,128]{1,0:T(8,128)(2,1)}, u32[]{:S(2)}) copy-start(bf16[128,128]{1,0:T(8,128)(2,1)} %param.17) | copy-start | bytes 98308
  713.4 3.3 copy-start.4
  717.8 0.9 copy-start.1
Sparse Core Ops, SparseCore 0:
  13.4 137.7 all-gather.2
  182.1 230.4 reduce-scatter.2
  421.0 147.2 all-gather.4
  606.4 106.9 reduce-scatter.4
where the time goes:
time: 727 us; the launch traced here: 725 us
  waiting for transfers between devices  618 us (85%)
  local copies, waits for them, and re-layouts  46.8 us (6%)
  matrix products  31.3 us (4%)
  other arithmetic  15.1 us (2%)
  between operations  13.5 us (2%)
    reduce_scatter x1, waiting for transfers between devices, body(): lax.psum_scatter(jnp.einsum('jkc,ikc->jic', sliced, first_factor, preferr...  230 us
    all_gather x1, waiting for transfers between devices, body(): collected = lax.all_gather(early_factor, 'col', axis=1, tiled=True)  145 us
    all_gather x1, waiting for transfers between devices, body(): gathered = lax.all_gather(second_factor, 'row', axis=0, tiled=True)  136 us
    reduce_scatter x1, waiting for transfers between devices, body(): lax.psum_scatter(jnp.einsum('kic,kjc->ijc', sliced, later_factor, preferr...  107 us
    dot_general x1, matrix products, body(): jnp.einsum('jkc,ikc->jic', sliced, first_factor, preferred_element_type=j...  16.8 us
  transfers between devices with their start and end apart: 4, of which 4 were waited for; matrix products, arithmetic and copies ran while one was open for 1% of the time, Pallas kernels for 0%

commit v1 on v0

v1 whole, which is shorter than its diff:
```python
import functools

import jax
import jax.numpy as jnp
from jax import lax
from jax.experimental import pallas as pl
from jax.experimental.pallas import tpu as pltpu
from jax.sharding import PartitionSpec as P

MESH = pl.DeviceIdType.MESH


def exchange_kernel(axis, n, x_ref, o_ref, send, recv, local):
    me = lax.axis_index(axis)
    barrier = pltpu.get_barrier_semaphore()

    def greet(s, carry):
        pl.semaphore_signal(
            barrier, inc=1, device_id={axis: lax.rem(me + s, n)}, device_id_type=MESH
        )
        return carry

    def copy(p, slot):
        return pltpu.make_async_remote_copy(
            src_ref=x_ref.at[p],
            dst_ref=o_ref.at[slot],
            send_sem=send.at[p],
            recv_sem=recv.at[slot],
            device_id={axis: p},
            device_id_type=MESH,
        )

    def start(s, carry):
        copy(lax.rem(me + s, n), me).start()
        return carry

    def finish(s, carry):
        p = lax.rem(me + s, n)
        landed = copy(p, p)
        landed.wait_recv()
        landed.wait_send()
        return carry

    lax.fori_loop(1, n, greet, 0)
    own = pltpu.make_async_copy(x_ref.at[me], o_ref.at[me], local)
    own.start()
    pl.semaphore_wait(barrier, n - 1)
    lax.fori_loop(1, n, start, 0)
    lax.fori_loop(1, n, finish, 0)
    own.wait()


def exchange(x, axis, call_id):
    n = x.shape[0]
    return pl.pallas_call(
        functools.partial(exchange_kernel, axis, n),
        out_shape=jax.ShapeDtypeStruct(x.shape, x.dtype),
        in_specs=[pl.BlockSpec(memory_space=pl.ANY)],
        out_specs=pl.BlockSpec(memory_space=pl.ANY),
        scratch_shapes=[
            pltpu.SemaphoreType.DMA((n,)),
            pltpu.SemaphoreType.DMA((n,)),
            pltpu.SemaphoreType.DMA,
        ],
        name=f"exchange_{axis}_{call_id}",
        compiler_params=pltpu.CompilerParams(collective_id=call_id, has_side_effects=True),
    )(x)


def normalize(values, gain, axis=-1):
    floated = values.astype(jnp.float32)
    center = jnp.mean(floated, axis=axis, keepdims=True)
    spread = jnp.mean((floated - center) ** 2, axis=axis, keepdims=True)
    return ((floated - center) * lax.rsqrt(spread + 1e-05) * gain).astype(jnp.bfloat16)


def update(field, gain, weights, scale, final, outgoing, ids):
    rows, cols, c = field.shape
    n_row, n_col = lax.axis_size("row"), lax.axis_size("col")
    per = c // n_col
    normed = normalize(field, gain).reshape(rows * cols, c)

    def turned(column):
        return lax.dot_general(
            weights[:, column * c : (column + 1) * c],
            normed,
            (((0,), (1,)), ((), ())),
            preferred_element_type=jnp.float32,
        )

    first = (jax.nn.sigmoid(turned(0)) * turned(1)).astype(jnp.bfloat16)
    second = (jax.nn.sigmoid(turned(2)) * turned(3)).astype(jnp.bfloat16)
    packed = jnp.concatenate(
        [first.reshape(n_col, per, -1), second.reshape(n_col, per, -1)], axis=1
    )
    swapped = exchange(packed, "col", ids)
    wide = (
        swapped.reshape(n_col, 2 * per, rows, cols)
        .transpose(1, 2, 0, 3)
        .reshape(2, per, rows, n_col * cols)
    )
    left, right = wide[0], wide[1]
    if outgoing:
        left = left.reshape(per * 2, rows // 2, n_col * cols)
        right = jnp.repeat(right, 2, axis=0)
        cut = rows // 2
        got = exchange(jnp.concatenate([left, right], axis=1), "row", ids + 1)
        lhs = got[:, :cut].reshape(-1, n_col * cols)
        rhs = got[:, cut:].reshape(-1, n_col * cols)
        product = lax.dot_general(
            lhs, rhs, (((1,), (1,)), ((), ())), preferred_element_type=jnp.float32
        ).astype(jnp.bfloat16)
        back = exchange(product.reshape(n_row, cut, n_col * cols), "row", ids + 2)
        back = back.reshape(per, rows, n_col, cols)
    else:
        half = n_col * cols // 2
        left = jnp.repeat(left, 2, axis=0)
        right = right.reshape(per, rows, 2, half).transpose(0, 2, 1, 3)
        right = right.reshape(per * 2, rows, half)
        got = exchange(jnp.concatenate([left, right], axis=2), "row", ids + 1)
        got = got.reshape(-1, 3 * half)
        product = lax.dot_general(
            got[:, : 2 * half],
            got[:, 2 * half :],
            (((0,), (0,)), ((), ())),
            preferred_element_type=jnp.float32,
        ).astype(jnp.bfloat16)
        back = exchange(product.reshape(n_row, rows, half), "row", ids + 2)
        back = back.reshape(per, 2, rows, half).transpose(0, 2, 1, 3)
        back = back.reshape(per, rows, n_col, cols)
    parts = back.transpose(2, 0, 1, 3).reshape(n_col, per, rows * cols)
    product = exchange(parts, "col", ids + 3).reshape(c, rows * cols)
    mixed = normalize(product, scale[:, None], axis=0)
    gating = jax.nn.sigmoid(
        jnp.dot(normed, weights[:, 4 * c :], preferred_element_type=jnp.float32)
    )
    change = gating * lax.dot_general(
        mixed, final, (((0,), (0,)), ((), ())), preferred_element_type=jnp.float32
    )
    return (field.astype(jnp.float32) + change.reshape(field.shape)).astype(jnp.bfloat16)


def body(state, n1, m1, s1, f1, n2, m2, s2, f2):
    middle = update(state, n1, m1, s1, f1, True, 1)
    return update(middle, n2, m2, s2, f2, False, 5)


def solution(mesh):
    placed = (P("row", "col", None), P(), P(), P(), P(), P(), P(), P(), P())
    return jax.shard_map(
        body, mesh=mesh, in_specs=placed, out_specs=P("row", "col", None), check_vma=False
    )
```

time: 727 us -> 274 us (0.38)
  waiting for transfers between devices: 618 us -> 0 us
  Pallas kernels: 0 us -> 204 us
  matrix products: 31.3 us -> 9.33 us
  between operations: 13.5 us -> 0.61 us
    reduce_scatter x2 -> x0, waiting for transfers between devices: 337 us -> none  [the longest x1 230 us: body(): lax.psum_scatter(jnp.einsum('jkc,ikc->jic', sliced, first_factor, preferr...]
    all_gather x2 -> x0, waiting for transfers between devices: 282 us -> none  [the longest x1 145 us: body(): collected = lax.all_gather(early_factor, 'col', axis=1, tiled=True)]
    pallas_call x0 -> x8, Pallas kernels: none -> 204 us  [exchange(): pl.pallas_call(functools.partial(exchange_kernel, axis, n), out_shape=jax...]
    convert_element_type x2 -> x4, local copies, waits for them, and re-layouts: 27.9 us -> 0.99 us  [the longest x2 0.49 us: update(): first = (jax.nn.sigmoid(turned(0)) * turned(1)).astype(jnp.bfloat16)]
    dot_general x14, matrix products: 31.3 us -> 9.33 us  [the longest x1 3.06 us: update(): lax.dot_general(got[:, :2 * half], got[:, 2 * half:], (((0,), (0,)), ((),...]
    reshape x4 -> x10, local copies, waits for them, and re-layouts: 4.75 us -> 25.5 us  [the longest x4 14.6 us: update(): swapped.reshape(n_col, 2 * per, rows, cols).transpose(1, 2, 0, 3)]
    all_gather x1 -> x0, local copies, waits for them, and re-layouts: 14 us -> none  [body(): collected = lax.all_gather(early_factor, 'col', axis=1, tiled=True)]
  transfers between devices with their start and end apart: 4 -> 0, of which waited for: 4 -> 0; matrix products, arithmetic and copies ran while one was open for 1% -> 0% of each run, Pallas kernels for 0% -> 0%
where the time goes in v1:
time: 274 us
  Pallas kernels  204 us (74%)
  local copies, waits for them, and re-layouts  42.8 us (16%)
  other arithmetic  16.6 us (6%)
  matrix products  9.33 us (3%)
    pallas_call x8, Pallas kernels, exchange(): pl.pallas_call(functools.partial(exchange_kernel, axis, n), out_shape=jax...  204 us
    reshape x4, local copies, waits for them, and re-layouts, update(): swapped.reshape(n_col, 2 * per, rows, cols).transpose(1, 2, 0, 3)  14.6 us

profile of v1, /device:TPU:1, one launch (start us, length us, event | category | flops | bytes accessed | tf_op | source)
XLA Modules:
  0.0 273.8 jit_solution(5492068863420240127)
XLA Ops:
  0.0 1.5 convert_reduce_fusion.3
  1.5 1.8 fusion.33
  3.4 0.8 fusion.35
  4.2 0.5 fusion.14
  5.2 0.5 fusion.11
  6.2 1.1 pad_maximum_fusion.2.x_ref
  7.3 37.9 %exchange_col_1.1 = bf16[16,16,2304]{2,1,0:T(8,128)(2,1)} custom-call(bf16[16,16,2304]{2,1,0:T(8,128)(2,1)} %pad_maximum_fusion.2.x_ref), custom_call_target="tpu_custom_call" | custom-call | tf_op jit(solution)/shard_map/exchange_col_1/pallas_call | solution.py:55
  45.2 5.3 %reshape.150 = bf16[16,16,48,48]{3,2,1,0:T(8,128)(2,1)S(1)} reshape(bf16[16,16,2304]{2,1,0:T(8,128)(2,1)} %exchange_col_1.1) | data formatting | bytes 2359296 | tf_op jit(solution)/shard_map/reshape | solution.py:98
  50.5 2.0 copy.55
  52.5 0.5 fusion.72
  53.1 2.3 squeeze.6
  55.3 1.1 broadcast_in_dim.4
  56.5 1.6 reshape_squeeze.6
  58.0 1.3 pad_maximum_fusion.x_ref
  59.4 28.0 %exchange_row_2.1 = bf16[16,72,768]{2,1,0:T(8,128)(2,1)} custom-call(bf16[16,72,768]{2,1,0:T(8,128)(2,1)} %pad_maximum_fusion.x_ref), custom_call_target="tpu_custom_call" | custom-call | tf_op jit(solution)/shard_map/exchange_row_2/pallas_call | solution.py:55
  87.4 1.0 slice-done.1
  88.9 1.5 convolution_convert_fusion.1
  90.3 16.8 %exchange_row_3.1 = bf16[16,24,768]{2,1,0:T(8,128)(2,1)} custom-call(bf16[16,24,768]{2,1,0:T(8,128)(2,1)} %bitcast.116), custom_call_target="tpu_custom_call" | custom-call | tf_op jit(solution)/shard_map/exchange_row_3/pallas_call | solution.py:55
  107.2 2.8 %reshape.155 = bf16[8,48,16,48]{3,2,1,0:T(8,128)(2,1)S(1)} reshape(bf16[16,24,768]{2,1,0:T(8,128)(2,1)} %exchange_row_3.1) | data formatting | bytes 1179648 | tf_op jit(solution)/shard_map/reshape | solution.py:114
  110.4 2.3 reshape.156.x_ref
  112.7 21.9 %exchange_col_4.1 = bf16[16,8,2304]{2,1,0:T(8,128)(2,1)} custom-call(bf16[16,8,2304]{2,1,0:T(8,128)(2,1)} %reshape.156.x_ref), custom_call_target="tpu_custom_call" | custom-call | tf_op jit(solution)/shard_map/exchange_col_4/pallas_call | solution.py:55
  134.6 1.2 convert_reduce_fusion.1
  135.7 1.2 fusion.43
  137.5 0.6 copy-done.2
  138.5 0.6 copy-done.5
  139.6 0.7 fusion.30
  140.3 0.8 fusion.32
  143.2 1.1 pad_maximum_fusion.3.x_ref
  144.3 33.3 %exchange_col_5.1 = bf16[16,16,2304]{2,1,0:T(8,128)(2,1)} custom-call(bf16[16,16,2304]{2,1,0:T(8,128)(2,1)} %pad_maximum_fusion.3.x_ref), custom_call_target="tpu_custom_call" | custom-call | tf_op jit(solution)/shard_map/exchange_col_5/pallas_call | solution.py:55
  177.6 5.3 %reshape.161 = bf16[16,16,48,48]{3,2,1,0:T(8,128)(2,1)S(1)} reshape(bf16[16,16,2304]{2,1,0:T(8,128)(2,1)} %exchange_col_5.1) | data formatting | bytes 2359296 | tf_op jit(solution)/shard_map/reshape | solution.py:98
  182.9 2.0 copy.54
  184.9 0.5 fusion.71
  185.5 2.3 squeeze.7
  187.7 1.1 broadcast_in_dim.5
  188.9 2.5 reshape_squeeze.7
  191.5 1.3 pad_maximum_fusion.1.x_ref
  192.9 28.1 %exchange_row_6.1 = bf16[16,48,1152]{2,1,0:T(8,128)(2,1)} custom-call(bf16[16,48,1152]{2,1,0:T(8,128)(2,1)} %pad_maximum_fusion.1.x_ref), custom_call_target="tpu_custom_call" | custom-call | tf_op jit(solution)/shard_map/exchange_row_6/pallas_call | solution.py:55
  221.0 3.1 %convolution_convert_fusion = bf16[768,384]{1,0:T(8,128)(2,1)} fusion(bf16[768,1152]{1,0:T(8,128)(2,1)} %bitcast.115), kind=kOutput, calls=%fused_computation.59 | convolution fusion | flops 453279744 | bytes 2359296 | tf_op jit(solution)/shard_map/dot_general | solution.py:122
  224.0 16.6 %exchange_row_7.1 = bf16[16,48,384]{2,1,0:T(8,128)(2,1)} custom-call(bf16[16,48,384]{2,1,0:T(8,128)(2,1)} %bitcast.117), custom_call_target="tpu_custom_call" | custom-call | tf_op jit(solution)/shard_map/exchange_row_7/pallas_call | solution.py:55
  240.6 1.5 copy.57
  242.1 1.6 reshape.167
  244.1 2.3 reshape.168.x_ref
  246.4 21.9 %exchange_col_8.1 = bf16[16,8,2304]{2,1,0:T(8,128)(2,1)} custom-call(bf16[16,8,2304]{2,1,0:T(8,128)(2,1)} %reshape.168.x_ref), custom_call_target="tpu_custom_call" | custom-call | tf_op jit(solution)/shard_map/exchange_col_8/pallas_call | solution.py:55
  268.3 1.2 convert_reduce_fusion
  269.5 1.2 fusion.49
  271.2 0.6 copy-done.3
  272.3 0.6 copy-done.7
  272.9 0.9 fusion.37
  (63 shorter events, 6.7 us)
Async XLA Ops:
  0.0 137.5 %copy-start = (bf16[128,128]{1,0:T(8,128)(2,1)S(1)}, bf16[128,128]{1,0:T(8,128)(2,1)}, u32[]{:S(2)}) copy-start(bf16[128,128]{1,0:T(8,128)(2,1)} %param.13) | copy-start | bytes 98308
  0.0 3.3 %copy-start.4 = (bf16[48,48,128]{2,1,0:T(8,128)(2,1)S(1)}, bf16[48,48,128]{2,1,0:T(8,128)(2,1)}, u32[]{:S(2)}) copy-start(bf16[48,48,128]{2,1,0:T(8,128)(2,1)} %param.9) | copy-start | bytes 1769476
  0.0 3.3 %copy-start.15 = (f32[128]{0:T(128)S(1)}, f32[128]{0:T(128)}, u32[]{:S(2)}) copy-start(f32[128]{0:T(128)} %param.10) | copy-start | bytes 1540
  0.0 4.1 %copy-start.13 = (bf16[128,640]{1,0:T(8,128)(2,1)S(1)}, bf16[128,640]{1,0:T(8,128)(2,1)}, u32[]{:S(2)}) copy-start(bf16[128,640]{1,0:T(8,128)(2,1)} %param.11) | copy-start | bytes 491524
  4.1 1.5 copy-start.8
  87.4 1.1 slice-start.1
  87.4 1.4 slice-start
  112.7 24.3 %copy-start.9 = (bf16[48,48,128]{2,1,0:T(8,128)(2,1)S(1)}, bf16[48,48,128]{2,1,0:T(8,128)(2,1)}, u32[]{:S(2)}) copy-start(bf16[48,48,128]{2,1,0:T(8,128)(2,1)} %copy-done.8) | copy-start | bytes 1769476
  137.0 1.1 copy-start.2
  137.0 1.1 copy-start.16
  138.1 1.1 copy-start.5
  139.1 1.2 copy-start.17
  139.5 2.1 copy-start.6
  139.5 1.6 copy-start.14
  141.1 1.5 copy-start.10
  246.4 24.3 %copy-start.11 = (bf16[48,48,128]{2,1,0:T(8,128)(2,1)S(1)}, bf16[48,48,128]{2,1,0:T(8,128)(2,1)}, u32[]{:S(2)}) copy-start(bf16[48,48,128]{2,1,0:T(8,128)(2,1)} %copy-done.10) | copy-start | bytes 1769476
  270.7 1.1 copy-start.3
  270.7 1.1 copy-start.12
  270.8 1.0 copy-start.18
  271.8 1.1 copy-start.7
  272.3 1.6 copy-start.1

commit v2 on v0

v2 whole, which is shorter than its diff:
```python
import functools

import jax
import jax.numpy as jnp
from jax import lax
from jax.experimental import pallas as pl
from jax.experimental.pallas import tpu as pltpu
from jax.sharding import PartitionSpec as P

MESH = pl.DeviceIdType.MESH
N_ROW, N_COL, T, C = 16, 16, 48, 128
PER = C // N_COL
N = N_ROW * T
IH, TH = T // 8, T // 16
LANES = TH * 128
F32, BF16 = jnp.float32, jnp.bfloat16
NT = (((1,), (1,)), ((), ()))
TN = (((0,), (0,)), ((), ()))


def normalize(x, axis):
    center = jnp.mean(x, axis=axis, keepdims=True)
    spread = jnp.mean((x - center) ** 2, axis=axis, keepdims=True)
    return (x - center) * lax.rsqrt(spread + 1e-05)


def block_transpose(v):
    block = lax.broadcasted_iota(jnp.int32, v[0].shape, 1) // 16
    for step in (1, 2, 4):
        low = (block & step) == 0
        out = list(v)
        for a in range(8):
            if a & step == 0:
                x, y = v[a], v[a + step]
                out[a] = jnp.where(low, x, pltpu.roll(y, 16 * step, 1))
                out[a + step] = jnp.where(low, pltpu.roll(x, 128 - 16 * step, 1), y)
        v = out
    return v


def kernel(
    outgoing,
    z_ref, gain_ref, w_ref, scale_ref, final_ref,
    out_ref,
    wt, normed, gate, scale_t,
    send1, got1, wide, send2, left, right, send3, got3, wide3, send4, got4,
    s1, r1, s2a, r2a, s2b, r2b, sf, s3, r3, s4, r4, local,
):
    row, col = lax.axis_index("row"), lax.axis_index("col")
    chan, half = row // 2, row % 2
    barrier = pltpu.get_barrier_semaphore()

    def each(first, last, body):
        def step(s, carry):
            body(s)
            return carry

        lax.fori_loop(first, last, step, 0)

    def greet(s):
        pl.semaphore_signal(
            barrier, inc=1, device_id={"row": lax.rem(row + s, N_ROW)}, device_id_type=MESH
        )
        pl.semaphore_signal(
            barrier, inc=1, device_id={"col": lax.rem(col + s, N_COL)}, device_id_type=MESH
        )

    each(1, 16, greet)

    def remote(src, dst, send, recv, axis, peer):
        return pltpu.make_async_remote_copy(
            src_ref=src, dst_ref=dst, send_sem=send, recv_sem=recv,
            device_id={axis: peer}, device_id_type=MESH,
        )

    wt[...] = jnp.transpose(w_ref[...].astype(F32)).astype(BF16)
    scale_t[...] = jnp.transpose(jnp.broadcast_to(scale_ref[...], (C, C)))

    def project(array, ih):
        x = normed[pl.ds(pl.multiple_of(ih * LANES, LANES), LANES), :]
        base = 2 * C * array
        g = lax.dot_general(wt[base : base + C, :], x, NT, preferred_element_type=F32)
        v = lax.dot_general(wt[base + C : base + 2 * C, :], x, NT, preferred_element_type=F32)
        made = jax.nn.sigmoid(g) * v
        send1[array, :, pl.ds(ih, 1)] = made.reshape(N_COL, 1, PER, LANES).astype(BF16)

    def prepare(ih):
        lines = pl.ds(pl.multiple_of(ih * 8, 8), 8)
        x = jnp.concatenate(
            [z_ref[lines, 16 * t : 16 * t + 16, :].reshape(128, C) for t in range(TH)], axis=0
        ).astype(F32)
        x = (normalize(x, 1) * gain_ref[...]).astype(BF16)
        normed[pl.ds(pl.multiple_of(ih * LANES, LANES), LANES), :] = x
        project(0, ih)

    each(0, IH, prepare)

    def col1(array, peer, slot):
        return remote(
            send1.at[array, peer], got1.at[array, slot],
            s1.at[array, peer], r1.at[array, slot], "col", peer,
        )

    def own1(array):
        return pltpu.make_async_copy(
            send1.at[array, col], got1.at[array, col], local.at[array]
        )

    pl.semaphore_wait(barrier, 30)
    each(1, N_COL, lambda s: col1(0, lax.rem(col + s, N_COL), col).start())
    own1(0).start()
    each(0, IH, lambda ih: project(1, ih))
    each(1, N_COL, lambda s: col1(1, lax.rem(col + s, N_COL), col).start())
    own1(1).start()

    def gating(ih):
        lines = pl.ds(pl.multiple_of(ih * LANES, LANES), LANES)
        gate[lines, :] = jax.nn.sigmoid(
            jnp.dot(normed[lines, :], w_ref[:, 4 * C :], preferred_element_type=F32)
        )

    each(0, IH, gating)

    def widen(array):
        def landed(s):
            peer = lax.rem(col + s, N_COL)
            col1(array, peer, peer).wait_recv()

        each(1, N_COL, landed)
        own1(array).wait()
        for u in range(2):
            for t in range(TH):
                v = [
                    got1[array, 8 * u + q, :, :, 128 * t : 128 * t + 128]
                    .astype(F32)
                    .reshape(IH * PER, 128)
                    for q in range(8)
                ]
                tile = u * TH + t
                for il, w in enumerate(block_transpose(v)):
                    for ih in range(IH):
                        wide[tile, ih * 64 + il * 8 : ih * 64 + il * 8 + 8] = w[
                            ih * 8 : ih * 8 + 8
                        ]

        for c in range(PER):
            for tile in range(2 * TH):
                send2[array, c, :, :, 128 * tile : 128 * tile + 128] = (
                    wide[tile, pl.ds(c, T, stride=8), :].astype(BF16).reshape(TH, 16, 128)
                )

    def place(ref, source):
        return ref.at[source // 8, :, lax.rem(source, 8)]

    if outgoing:
        sources_a, upper = 8, row // 8

        def pair_a(c, source):
            return send2.at[0, c], left.at[lax.rem(source, 8)], 2 * c + source // 8

    else:
        sources_a, upper = 16, 0

        def pair_a(s, source):
            c, h = s // 2, lax.rem(s, 2)
            cut = pl.ds(pl.multiple_of(h * LANES, LANES), LANES)
            return send2.at[0, c, :, :, cut], place(left, source), s

    def send_a(s):
        src, dst, peer = pair_a(s, row)

        @pl.when(peer != row)
        def _():
            remote(src, dst, s2a.at[s], r2a.at[row], "row", peer).start()

        @pl.when(peer == row)
        def _():
            pltpu.make_async_copy(src, dst, r2a.at[row]).start()

    def sent_a(s):
        src, dst, peer = pair_a(s, row)

        @pl.when(peer != row)
        def _():
            remote(src, dst, s2a.at[s], r2a.at[row], "row", peer).wait_send()

    def take_a(s):
        source = half * 8 + s if outgoing else s
        src, dst, peer = pair_a(0, source)

        @pl.when(source != row)
        def _():
            remote(src, dst, s2a.at[0], r2a.at[source], "row", source).wait_recv()

        @pl.when(source == row)
        def _():
            pltpu.make_async_copy(src, dst, r2a.at[source]).wait()

    widen(0)
    each(0, sources_a, send_a)

    def copy_b(c, source, peer):
        return remote(
            send2.at[1, c], place(right, source), s2b.at[c], r2b.at[source], "row", peer
        )

    def own_b():
        return pltpu.make_async_copy(send2.at[1, chan], place(right, row), r2b.at[row])

    partner = chan * 2 + (1 - half)

    def hand(source):
        return remote(
            place(right, source), place(right, source), sf.at[source], r2b.at[source],
            "row", partner,
        )

    def send_b(s):
        c = lax.rem(chan + s, PER)
        copy_b(c, row, 2 * c + half).start()

    widen(1)
    own_b().start()
    each(1, PER, send_b)
    each(0, sources_a, take_a)

    def pass_on(s):
        c = lax.rem(chan + s, PER)
        source = 2 * c + half
        copy_b(c, source, source).wait_recv()
        hand(source).start()

    own_b().wait()
    hand(row).start()
    each(1, PER, pass_on)

    def take_b(c):
        source = 2 * c + (1 - half)
        hand(source).wait_recv()

    each(0, PER, take_b)

    def copy3(m, s, peer, slot):
        return remote(
            send3.at[m, s], got3.at[m, slot], s3.at[m, s], r3.at[m, slot], "row", peer
        )

    def own3(m):
        return pltpu.make_async_copy(
            send3.at[m, lax.rem(row, 8)], got3.at[m, chan], r3.at[m, chan]
        )

    mine = row // 8 == half
    for m in range(TH):
        if outgoing:
            made = lax.dot_general(
                left[:, m].reshape(128, N), right[...].reshape(N, N), NT,
                preferred_element_type=F32,
            )
        else:
            made = lax.dot_general(
                left[:, :, :, :, 128 * m : 128 * m + 128].reshape(N, 128),
                right[...].reshape(N, N), TN, preferred_element_type=F32,
            )
        send3[m] = made.astype(BF16).reshape(8, 16, N)

        def send_p(s):
            peer = half * 8 + s

            @pl.when(peer != row)
            def _():
                copy3(m, s, peer, chan).start()

        each(0, 8, send_p)

        @pl.when(mine)
        def _():
            own3(m).start()

    def col4(m, peer, slot):
        return remote(
            send4.at[peer, pl.ds(2 * m, 2)], got4.at[slot, pl.ds(2 * m, 2)],
            s4.at[m, peer], r4.at[m, slot], "col", peer,
        )

    def own4(m):
        return pltpu.make_async_copy(
            send4.at[col, pl.ds(2 * m, 2)], got4.at[col, pl.ds(2 * m, 2)], local.at[2 + m]
        )

    for m in range(TH):

        def take_p(c):
            source = 2 * c + row // 8

            @pl.when(source != row)
            def _():
                copy3(m, 0, source, c).wait_recv()

            @pl.when(source == row)
            def _():
                own3(m).wait()

        each(0, PER, take_p)
        for c in range(PER):
            for tile in range(2 * TH):
                wide3[tile, pl.ds(c, 16, stride=8), :] = got3[
                    m, c, :, 128 * tile : 128 * tile + 128
                ].astype(F32)
        for u in range(2):
            for t in range(TH):
                tile = u * TH + t
                v = [
                    jnp.concatenate(
                        [
                            wide3[tile, ih * 64 + il * 8 : ih * 64 + il * 8 + 8]
                            for ih in range(2)
                        ],
                        axis=0,
                    )
                    for il in range(8)
                ]
                for q, w in enumerate(block_transpose(v)):
                    send4[8 * u + q, 2 * m : 2 * m + 2, :, 128 * t : 128 * t + 128] = w.reshape(
                        2, PER, 128
                    ).astype(BF16)
        each(1, N_COL, lambda s: col4(m, lax.rem(col + s, N_COL), col).start())
        own4(m).start()

    for m in range(TH):

        def landed4(s):
            peer = lax.rem(col + s, N_COL)
            col4(m, peer, peer).wait_recv()

        each(1, N_COL, landed4)
        own4(m).wait()

        def finish(ih):
            lines = pl.ds(pl.multiple_of(ih * 8, 8), 8)
            x = got4[:, pl.ds(ih, 1)].astype(F32).reshape(C, LANES)
            x = normalize(x, 0) * jnp.concatenate([scale_t[...]] * TH, axis=1)
            change = lax.dot_general(
                x.astype(BF16), final_ref[...], TN, preferred_element_type=F32
            )
            change = change * gate[pl.ds(pl.multiple_of(ih * LANES, LANES), LANES), :]
            for t in range(TH):
                there = z_ref[lines, 16 * t : 16 * t + 16, :].astype(F32)
                there = there + change[128 * t : 128 * t + 128].reshape(8, 16, C)
                out_ref[lines, 16 * t : 16 * t + 16, :] = there.astype(BF16)

        each(2 * m, 2 * m + 2, finish)

    for array in range(2):
        each(
            1, N_COL,
            lambda s: col1(array, lax.rem(col + s, N_COL), col).wait_send(),
        )
    each(0, sources_a, sent_a)
    each(1, PER, lambda s: copy_b(lax.rem(chan + s, PER), row, row).wait_send())
    each(0, PER, lambda c: hand(2 * c + half).wait_send())
    for m in range(TH):

        def sent_p(s):
            peer = half * 8 + s

            @pl.when(peer != row)
            def _():
                copy3(m, s, peer, chan).wait_send()

        each(0, 8, sent_p)
        each(1, N_COL, lambda s: col4(m, lax.rem(col + s, N_COL), col).wait_send())


def update(field, gain, weights, scale, final, outgoing, call_id):
    vm = pltpu.VMEM
    dma = pltpu.SemaphoreType.DMA
    left = (8, TH, 16, N) if outgoing else (2, TH, 8, 16, LANES)
    return pl.pallas_call(
        functools.partial(kernel, outgoing),
        out_shape=jax.ShapeDtypeStruct(field.shape, field.dtype),
        scratch_shapes=[
            vm((5 * C, C), BF16),
            vm((T * T, C), BF16),
            vm((T * T, C), F32),
            vm((C, C), F32),
            vm((2, N_COL, IH, PER, LANES), BF16),
            vm((2, N_COL, IH, PER, LANES), BF16),
            vm((2 * TH, T * PER, 128), F32),
            vm((2, PER, TH, 16, N), BF16),
            vm(left, BF16),
            vm((2, TH, 8, 16, N), BF16),
            vm((TH, 8, 16, N), BF16),
            vm((TH, PER, 16, N), BF16),
            vm((2 * TH, 16 * PER, 128), F32),
            vm((N_COL, IH, PER, LANES), BF16),
            vm((N_COL, IH, PER, LANES), BF16),
            dma((2, N_COL)), dma((2, N_COL)),
            dma((N_ROW,)), dma((N_ROW,)),
            dma((PER,)), dma((N_ROW,)), dma((N_ROW,)),
            dma((TH, 8)), dma((TH, PER)),
            dma((TH, N_COL)), dma((TH, N_COL)),
            dma((2 + TH,)),
        ],
        name="outgoing" if outgoing else "incoming",
        compiler_params=pltpu.CompilerParams(collective_id=call_id, has_side_effects=True),
    )(field, gain.reshape(1, C), weights, scale.reshape(1, C), final)


def body(state, n1, m1, s1, f1, n2, m2, s2, f2):
    middle = update(state, n1, m1, s1, f1, True, 1)
    return update(middle, n2, m2, s2, f2, False, 2)


def solution(mesh):
    placed = (P("row", "col", None), P(), P(), P(), P(), P(), P(), P(), P())
    return jax.shard_map(
        body, mesh=mesh, in_specs=placed, out_specs=P("row", "col", None), check_vma=False
    )
```

time: 727 us -> 155 us (0.21)
  waiting for transfers between devices: 618 us -> 0 us
  Pallas kernels: 0 us -> 153 us
  local copies, waits for them, and re-layouts: 46.8 us -> 1.92 us
  matrix products: 31.3 us -> 0 us
  other arithmetic: 15.1 us -> 0 us
  between operations: 13.5 us -> 0.02 us
    reduce_scatter x2 -> x0, waiting for transfers between devices: 337 us -> none  [the longest x1 230 us: body(): lax.psum_scatter(jnp.einsum('jkc,ikc->jic', sliced, first_factor, preferr...]
    all_gather x2 -> x0, waiting for transfers between devices: 282 us -> none  [the longest x1 145 us: body(): collected = lax.all_gather(early_factor, 'col', axis=1, tiled=True)]
    pallas_call x0 -> x2, Pallas kernels: none -> 153 us  [update(): pl.pallas_call(functools.partial(kernel, outgoing), out_shape=jax.ShapeDt...]
    dot_general x14 -> x0, matrix products: 31.3 us -> none  [the longest x1 16.8 us: body(): jnp.einsum('jkc,ikc->jic', sliced, first_factor, preferred_element_type=j...]
    convert_element_type x2 -> x0, local copies, waits for them, and re-layouts: 27.9 us -> none  [the longest x1 14 us: body(): jnp.einsum('jkc,ikc->jic', sliced, first_factor, preferred_element_type=j...]
    all_gather x1 -> x0, local copies, waits for them, and re-layouts: 14 us -> none  [body(): collected = lax.all_gather(early_factor, 'col', axis=1, tiled=True)]
    reduce_sum x8 -> x0, other arithmetic: 10.9 us -> none  [the longest x4 5.98 us: normalize(): spread = jnp.mean((floated - center) ** 2, axis=-1, keepdims=True)]
  transfers between devices with their start and end apart: 4 -> 0, of which waited for: 4 -> 0; matrix products, arithmetic and copies ran while one was open for 1% -> 0% of each run, Pallas kernels for 0% -> 0%
where the time goes in v2:
time: 155 us
  Pallas kernels  153 us (99%)
  local copies, waits for them, and re-layouts  1.92 us (1%)
    pallas_call x2, Pallas kernels, update(): pl.pallas_call(functools.partial(kernel, outgoing), out_shape=jax.ShapeDt...  153 us

profile of v2, /device:TPU:1, one launch (start us, length us, event | category | flops | bytes accessed | tf_op | source)
XLA Modules:
  0.0 154.6 jit_solution(11662293351065776496)
XLA Ops:
  0.0 78.5 %outgoing.1.z_ref = bf16[48,48,128]{2,1,0:T(8,128)(2,1)} custom-call(bf16[48,48,128]{2,1,0:T(8,128)(2,1)} %z_ref.1, f32[1,128]{1,0:T(1,128)} %bitcast.4, bf16[128,640]{1,0:T(8,128)(2,1)} %w_ref.2, f32[1,128]{1,0:T(1,128)} %bitcast.5, bf16[128,128]{1,0:T(8,128)(2,1)} %final_ref.2), custom_call_target="tpu_custom_call" | custom-call | tf_op jit(solution)/shard_map/outgoing/pallas_call | solution.py:379
  78.6 74.1 %incoming.1 = bf16[48,48,128]{2,1,0:T(8,128)(2,1)} custom-call(bf16[48,48,128]{2,1,0:T(8,128)(2,1)} %outgoing.1.z_ref, f32[1,128]{1,0:T(1,128)} %bitcast.6, bf16[128,640]{1,0:T(8,128)(2,1)} %w_ref.3, f32[1,128]{1,0:T(1,128)} %bitcast.7, bf16[128,128]{1,0:T(8,128)(2,1)} %final_ref.3), custom_call_target="tpu_custom_call" | custom-call | tf_op jit(solution)/shard_map/incoming/pallas_call | solution.py:379
  152.7 1.9 %copy.11 = bf16[48,48,128]{2,1,0:T(8,128)(2,1)} copy(bf16[48,48,128]{2,1,0:T(8,128)(2,1)} %incoming.1) | data formatting | bytes 1179648

commit v3 on v0

v3 whole, which is shorter than its diff:
```python
import jax
import jax.numpy as jnp
from jax import lax
from jax.experimental import pallas as pl
from jax.experimental.pallas import tpu as pltpu
from jax.sharding import PartitionSpec as P

MESH = pl.DeviceIdType.MESH
N_ROW, N_COL, T, C = 16, 16, 48, 128
PER = C // N_COL
N = N_ROW * T
IH, TH = T // 8, T // 16
LANES = TH * 128
F32, BF16 = jnp.float32, jnp.bfloat16
NT = (((1,), (1,)), ((), ()))
TN = (((0,), (0,)), ((), ()))


def normalize(x, axis):
    center = jnp.mean(x, axis=axis, keepdims=True)
    spread = jnp.mean((x - center) ** 2, axis=axis, keepdims=True)
    return (x - center) * lax.rsqrt(spread + 1e-05)


def block_transpose(v):
    block = lax.broadcasted_iota(jnp.int32, v[0].shape, 1) // 16
    for step in (1, 2, 4):
        low = (block & step) == 0
        out = list(v)
        for a in range(8):
            if a & step == 0:
                x, y = v[a], v[a + step]
                out[a] = jnp.where(low, x, pltpu.roll(y, 16 * step, 1))
                out[a + step] = jnp.where(low, pltpu.roll(x, 128 - 16 * step, 1), y)
        v = out
    return v


def each(first, last, body):
    def step(s, carry):
        body(s)
        return carry

    lax.fori_loop(first, last, step, 0)


def lines_of(ih):
    return pl.ds(pl.multiple_of(ih * LANES, LANES), LANES)


def remote(src, dst, send, recv, axis, peer):
    return pltpu.make_async_remote_copy(
        src_ref=src, dst_ref=dst, send_sem=send, recv_sem=recv,
        device_id={axis: peer}, device_id_type=MESH,
    )


BUFFERS = (
    "wt", "normed", "gate", "scale_t", "field",
    "send_b", "got_b", "send_a", "got_a",
    "row_b", "right", "row_a", "left", "send_p", "got_p", "send_o", "got_o",
    "sb1", "rb1", "sa1", "ra1", "sb2", "rb2", "sf", "sa2", "ra2",
    "s3", "r3", "s4", "r4", "local",
)


def buffers(outgoing):
    vm, dma = pltpu.VMEM, pltpu.SemaphoreType.DMA
    rows = (TH, N_COL, 2, PER, LANES)
    first = rows if outgoing else (TH, N_COL, IH, PER, 128)
    return [
        vm((5 * C, C), BF16), vm((T * T, C), BF16), vm((T * T, C), F32), vm((C, C), F32),
        vm((T * T, C), BF16),
        vm(rows, BF16), vm(rows, BF16), vm(first, BF16), vm(first, BF16),
        vm((TH, PER, 16, N), BF16), vm((2, TH, 8, 16, N), BF16),
        vm((TH, PER, 16, N) if outgoing else (TH, PER, 2, TH, 16, 128), BF16),
        vm((TH, 8, 16, N) if outgoing else (TH, 2, TH, 8, 16, 128), BF16),
        vm((TH, 8, 16, N), BF16), vm((TH, PER, 16, N), BF16),
        vm(rows, BF16), vm(rows, BF16),
        dma((TH, N_COL)), dma((TH, N_COL)), dma((TH, N_COL)), dma((TH, N_COL)),
        dma((TH, PER)), dma((TH, N_ROW)), dma((TH, PER)),
        dma((TH, N_ROW)), dma((TH, N_ROW)),
        dma((TH, 8)), dma((TH, PER)),
        dma((TH, N_COL)), dma((TH, N_COL)),
        dma((3, TH)),
    ]


class Update:
    def __init__(self, outgoing, wide, gain, weights, scale, final, refs):
        self.outgoing, self.wide = outgoing, wide
        self.gain, self.weights, self.scale, self.final = gain, weights, scale, final
        self.__dict__.update(zip(BUFFERS, refs))
        self.row, self.col = lax.axis_index("row"), lax.axis_index("col")
        self.chan, self.half = self.row // 2, self.row % 2

    def ready(self):
        self.wt[...] = jnp.transpose(self.weights[...].astype(F32)).astype(BF16)
        self.scale_t[...] = jnp.transpose(jnp.broadcast_to(self.scale[...], (C, C)))

    def prepare(self, ih):
        x = self.field[lines_of(ih), :].astype(F32)
        self.normed[lines_of(ih), :] = (normalize(x, 1) * self.gain[...]).astype(BF16)

    def project(self, array, ih):
        x, base = self.normed[lines_of(ih), :], 2 * C * array
        g = lax.dot_general(self.wt[base : base + C, :], x, NT, preferred_element_type=F32)
        v = lax.dot_general(
            self.wt[base + C : base + 2 * C, :], x, NT, preferred_element_type=F32
        )
        return jax.nn.sigmoid(g) * v

    def make_b(self, m):
        for e in range(2):
            made = self.project(1, 2 * m + e)
            self.send_b[m, :, e] = made.reshape(N_COL, PER, LANES).astype(BF16)

    def make_a(self, m):
        for e in range(2):
            made = self.project(0, 2 * m + e)
            if self.outgoing:
                self.send_a[m, :, e] = made.reshape(N_COL, PER, LANES).astype(BF16)
            else:
                for t in range(TH):
                    piece = made[:, 128 * t : 128 * t + 128].reshape(N_COL, PER, 128)
                    self.send_a[t, :, 2 * m + e] = piece.astype(BF16)

    def gating(self, ih):
        self.gate[lines_of(ih), :] = jax.nn.sigmoid(
            jnp.dot(
                self.normed[lines_of(ih), :], self.weights[:, 4 * C :],
                preferred_element_type=F32,
            )
        )

    def col_copy(self, sets, m, peer, slot):
        src, dst, send, recv, _ = sets
        return remote(
            src.at[m, peer], dst.at[m, slot], send.at[m, peer], recv.at[m, slot], "col", peer
        )

    def col_own(self, sets, m):
        src, dst, _, _, k = sets
        return pltpu.make_async_copy(
            src.at[m, self.col], dst.at[m, self.col], self.local.at[k, m]
        )

    def col_start(self, sets, m):
        each(
            1, N_COL,
            lambda s: self.col_copy(sets, m, lax.rem(self.col + s, N_COL), self.col).start(),
        )
        self.col_own(sets, m).start()

    def col_take(self, sets, m):
        def landed(s):
            peer = lax.rem(self.col + s, N_COL)
            self.col_copy(sets, m, peer, peer).wait_recv()

        each(1, N_COL, landed)
        self.col_own(sets, m).wait()

    def col_sent(self, sets, m):
        each(
            1, N_COL,
            lambda s: self.col_copy(
                sets, m, lax.rem(self.col + s, N_COL), self.col
            ).wait_send(),
        )

    @property
    def set_b(self):
        return self.send_b, self.got_b, self.sb1, self.rb1, 0

    @property
    def set_a(self):
        return self.send_a, self.got_a, self.sa1, self.ra1, 1

    @property
    def set_o(self):
        return self.send_o, self.got_o, self.s4, self.r4, 2

    def widen_rows(self, got, out, m):
        def side(u):
            for t in range(TH):
                v = [
                    got[m, 8 * u + q, :, :, 128 * t : 128 * t + 128]
                    .astype(F32)
                    .reshape(2 * PER, 128)
                    for q in range(8)
                ]
                for il, w in enumerate(block_transpose(v)):
                    for e in range(2):
                        self.wide[
                            u * TH + t, e * 64 + il * 8 : e * 64 + il * 8 + 8
                        ] = w[e * 8 : e * 8 + 8]

        each(0, 2, side)
        for c in range(PER):
            for tile in range(2 * TH):
                out[m, c, :, 128 * tile : 128 * tile + 128] = self.wide[
                    tile, pl.ds(c, 16, stride=8), :
                ].astype(BF16)

    def widen_lanes(self, got, out, t):
        def side(u):
            v = [
                got[t, 8 * u + q].astype(F32).reshape(IH * PER, 128) for q in range(8)
            ]
            for il, w in enumerate(block_transpose(v)):
                for ih in range(IH):
                    third, e = ih // 2, ih % 2
                    self.wide[
                        u * TH + third, e * 64 + il * 8 : e * 64 + il * 8 + 8
                    ] = w[ih * 8 : ih * 8 + 8]

        each(0, 2, side)
        for c in range(PER):
            for u in range(2):
                for third in range(TH):
                    out[t, c, u, third] = self.wide[
                        u * TH + third, pl.ds(c, 16, stride=8), :
                    ].astype(BF16)

    def place_b(self, m, source):
        return self.right.at[source // 8, m, lax.rem(source, 8)]

    def copy_b(self, m, c, source, peer):
        return remote(
            self.row_b.at[m, c], self.place_b(m, source), self.sb2.at[m, c],
            self.rb2.at[m, source], "row", peer,
        )

    def own_b(self, m):
        return pltpu.make_async_copy(
            self.row_b.at[m, self.chan], self.place_b(m, self.row), self.rb2.at[m, self.row]
        )

    def hand(self, m, source):
        there = self.place_b(m, source)
        return remote(
            there, there, self.sf.at[m, source // 2], self.rb2.at[m, source], "row",
            self.chan * 2 + (1 - self.half),
        )

    def spread_b(self, m):
        self.col_take(self.set_b, m)
        self.widen_rows(self.got_b, self.row_b, m)

        def send(s):
            c = lax.rem(self.chan + s, PER)
            self.copy_b(m, c, self.row, 2 * c + self.half).start()

        each(1, PER, send)
        self.own_b(m).start()

    def pass_b(self, m):
        def pass_on(s):
            c = lax.rem(self.chan + s, PER)
            source = 2 * c + self.half
            self.copy_b(m, c, source, source).wait_recv()
            self.hand(m, source).start()

        self.own_b(m).wait()
        self.hand(m, self.row).start()
        each(1, PER, pass_on)

    def take_b(self, m):
        each(0, PER, lambda c: self.hand(m, 2 * c + (1 - self.half)).wait_recv())

    def sent_b(self, m):
        each(
            1, PER,
            lambda s: self.copy_b(
                m, lax.rem(self.chan + s, PER), self.row, self.row
            ).wait_send(),
        )
        each(0, PER, lambda c: self.hand(m, 2 * c + self.half).wait_send())

    def pair_a(self, m, s, source):
        if self.outgoing:
            return self.row_a.at[m, s], self.left.at[m, lax.rem(source, 8)], 2 * s + source // 8
        there = self.left.at[m, source // 8, :, lax.rem(source, 8)]
        return self.row_a.at[m, s // 2, lax.rem(s, 2)], there, s

    def each_a(self, m, remote_step, own_step):
        def step(s):
            src, dst, peer = self.pair_a(m, s, self.row)

            @pl.when(peer != self.row)
            def _():
                remote_step(
                    remote(
                        src, dst, self.sa2.at[m, s], self.ra2.at[m, self.row], "row", peer
                    )
                )

            if own_step is not None:

                @pl.when(peer == self.row)
                def _():
                    own_step(pltpu.make_async_copy(src, dst, self.ra2.at[m, self.row]))

        each(0, 8 if self.outgoing else 16, step)

    def spread_a(self, m):
        self.col_take(self.set_a, m)
        if self.outgoing:
            self.widen_rows(self.got_a, self.row_a, m)
        else:
            self.widen_lanes(self.got_a, self.row_a, m)
        self.each_a(m, lambda copy: copy.start(), lambda copy: copy.start())

    def take_a(self, m):
        def step(s):
            source = self.half * 8 + s if self.outgoing else s
            src, dst, _ = self.pair_a(m, 0, source)

            @pl.when(source != self.row)
            def _():
                remote(
                    src, dst, self.sa2.at[m, 0], self.ra2.at[m, source], "row", source
                ).wait_recv()

            @pl.when(source == self.row)
            def _():
                pltpu.make_async_copy(src, dst, self.ra2.at[m, source]).wait()

        each(0, 8 if self.outgoing else 16, step)

    def sent_a(self, m):
        self.each_a(m, lambda copy: copy.wait_send(), None)

    def copy_p(self, m, s, peer, slot):
        return remote(
            self.send_p.at[m, s], self.got_p.at[m, slot], self.s3.at[m, s],
            self.r3.at[m, slot], "row", peer,
        )

    def own_p(self, m):
        return pltpu.make_async_copy(
            self.send_p.at[m, lax.rem(self.row, 8)], self.got_p.at[m, self.chan],
            self.r3.at[m, self.chan],
        )

    def multiply(self, m):
        right = self.right[...].reshape(N, N)
        if self.outgoing:
            made = lax.dot_general(
                self.left[m].reshape(128, N), right, NT, preferred_element_type=F32
            )
        else:
            made = lax.dot_general(
                self.left[m].reshape(N, 128), right, TN, preferred_element_type=F32
            )
        self.send_p[m] = made.astype(BF16).reshape(8, 16, N)

        def send(s):
            peer = self.half * 8 + s

            @pl.when(peer != self.row)
            def _():
                self.copy_p(m, s, peer, self.chan).start()

        each(0, 8, send)

        @pl.when(self.row // 8 == self.half)
        def _():
            self.own_p(m).start()

    def sent_p(self, m):
        def step(s):
            peer = self.half * 8 + s

            @pl.when(peer != self.row)
            def _():
                self.copy_p(m, s, peer, self.chan).wait_send()

        each(0, 8, step)

    def back(self, m):
        def take(c):
            source = 2 * c + self.row // 8

            @pl.when(source != self.row)
            def _():
                self.copy_p(m, 0, source, c).wait_recv()

            @pl.when(source == self.row)
            def _():
                self.own_p(m).wait()

        each(0, PER, take)
        for c in range(PER):
            for tile in range(2 * TH):
                self.wide[tile, pl.ds(c, 16, stride=8), :] = self.got_p[
                    m, c, :, 128 * tile : 128 * tile + 128
                ].astype(F32)

        def side(u):
            for t in range(TH):
                v = [
                    jnp.concatenate(
                        [
                            self.wide[u * TH + t, e * 64 + il * 8 : e * 64 + il * 8 + 8]
                            for e in range(2)
                        ],
                        axis=0,
                    )
                    for il in range(8)
                ]
                for q, w in enumerate(block_transpose(v)):
                    self.send_o[m, 8 * u + q, :, :, 128 * t : 128 * t + 128] = w.reshape(
                        2, PER, 128
                    ).astype(BF16)

        each(0, 2, side)
        self.col_start(self.set_o, m)

    def finish(self, m, e):
        ih = 2 * m + e
        x = self.got_o[m, :, e].astype(F32).reshape(C, LANES)
        x = normalize(x, 0) * jnp.concatenate([self.scale_t[...]] * TH, axis=1)
        change = lax.dot_general(
            x.astype(BF16), self.final[...], TN, preferred_element_type=F32
        )
        change = change * self.gate[lines_of(ih), :]
        return (self.field[lines_of(ih), :].astype(F32) + change).astype(BF16)

    def middle(self):
        self.spread_b(0)
        self.spread_b(1)
        self.pass_b(0)
        self.spread_b(2)
        self.pass_b(1)
        self.spread_a(0)
        self.pass_b(2)
        self.spread_a(1)
        for m in range(TH):
            self.take_b(m)
        self.take_a(0)
        self.multiply(0)
        self.spread_a(2)
        self.take_a(1)
        self.multiply(1)
        self.back(0)
        self.take_a(2)
        self.multiply(2)
        self.back(1)
        self.back(2)

    def sent(self):
        for m in range(TH):
            self.col_sent(self.set_b, m)
            self.col_sent(self.set_a, m)
            self.sent_b(m)
            self.sent_a(m)
            self.sent_p(m)
            self.col_sent(self.set_o, m)


def kernel(z_ref, n1, m1, s1, f1, n2, m2, s2, f2, out_ref, wide, *refs):
    count = len(refs) // 2
    one = Update(True, wide, n1, m1, s1, f1, refs[:count])
    two = Update(False, wide, n2, m2, s2, f2, refs[count:])
    barrier = pltpu.get_barrier_semaphore()

    def greet(s):
        for axis, place in (("row", one.row), ("col", one.col)):
            pl.semaphore_signal(
                barrier, inc=1, device_id={axis: lax.rem(place + s, 16)}, device_id_type=MESH
            )

    each(1, 16, greet)
    one.ready()
    for m in range(TH):

        def load(e):
            ih = 2 * m + e
            lines = pl.ds(pl.multiple_of(ih * 8, 8), 8)
            one.field[lines_of(ih), :] = jnp.concatenate(
                [z_ref[lines, 16 * t : 16 * t + 16, :].reshape(128, C) for t in range(TH)],
                axis=0,
            )
            one.prepare(ih)

        each(0, 2, load)
        one.make_b(m)
        if m == 0:
            pl.semaphore_wait(barrier, 30)
        one.col_start(one.set_b, m)
    for m in range(TH):
        one.make_a(m)
        one.col_start(one.set_a, m)
    each(0, IH, one.gating)
    two.ready()
    one.middle()
    for m in range(TH):
        one.col_take(one.set_o, m)

        def pass_on(e):
            ih = 2 * m + e
            two.field[lines_of(ih), :] = one.finish(m, e)
            two.prepare(ih)

        each(0, 2, pass_on)
        two.make_b(m)
        two.col_start(two.set_b, m)
    for m in range(TH):
        two.make_a(m)
    for m in range(TH):
        two.col_start(two.set_a, m)
    each(0, IH, two.gating)
    two.middle()
    for m in range(TH):
        two.col_take(two.set_o, m)

        def close(e):
            made = two.finish(m, e)
            lines = pl.ds(pl.multiple_of((2 * m + e) * 8, 8), 8)
            for t in range(TH):
                out_ref[lines, 16 * t : 16 * t + 16, :] = made[
                    128 * t : 128 * t + 128
                ].reshape(8, 16, C)

        each(0, 2, close)
    one.sent()
    two.sent()


def body(state, n1, m1, s1, f1, n2, m2, s2, f2):
    return pl.pallas_call(
        kernel,
        out_shape=jax.ShapeDtypeStruct(state.shape, state.dtype),
        scratch_shapes=[pltpu.VMEM((2 * TH, 16 * PER, 128), F32)]
        + buffers(True)
        + buffers(False),
        name="triangle",
        compiler_params=pltpu.CompilerParams(collective_id=1, has_side_effects=True),
    )(
        state,
        n1.reshape(1, C), m1, s1.reshape(1, C), f1,
        n2.reshape(1, C), m2, s2.reshape(1, C), f2,
    )


def solution(mesh):
    placed = (P("row", "col", None), P(), P(), P(), P(), P(), P(), P(), P())
    return jax.shard_map(
        body, mesh=mesh, in_specs=placed, out_specs=P("row", "col", None), check_vma=False
    )
```

time: 727 us -> 128 us (0.18)
  waiting for transfers between devices: 618 us -> 0 us
  Pallas kernels: 0 us -> 126 us
  local copies, waits for them, and re-layouts: 46.8 us -> 1.92 us
  matrix products: 31.3 us -> 0 us
  other arithmetic: 15.1 us -> 0 us
  between operations: 13.5 us -> 0.01 us
    reduce_scatter x2 -> x0, waiting for transfers between devices: 337 us -> none  [the longest x1 230 us: body(): lax.psum_scatter(jnp.einsum('jkc,ikc->jic', sliced, first_factor, preferr...]
    all_gather x2 -> x0, waiting for transfers between devices: 282 us -> none  [the longest x1 145 us: body(): collected = lax.all_gather(early_factor, 'col', axis=1, tiled=True)]
    pallas_call x0 -> x1, Pallas kernels: none -> 126 us  [body(): pl.pallas_call(kernel, out_shape=jax.ShapeDtypeStruct(state.shape, state....]
    dot_general x14 -> x0, matrix products: 31.3 us -> none  [the longest x1 16.8 us: body(): jnp.einsum('jkc,ikc->jic', sliced, first_factor, preferred_element_type=j...]
    convert_element_type x2 -> x0, local copies, waits for them, and re-layouts: 27.9 us -> none  [the longest x1 14 us: body(): jnp.einsum('jkc,ikc->jic', sliced, first_factor, preferred_element_type=j...]
    all_gather x1 -> x0, local copies, waits for them, and re-layouts: 14 us -> none  [body(): collected = lax.all_gather(early_factor, 'col', axis=1, tiled=True)]
    reduce_sum x8 -> x0, other arithmetic: 10.9 us -> none  [the longest x4 5.98 us: normalize(): spread = jnp.mean((floated - center) ** 2, axis=-1, keepdims=True)]
  transfers between devices with their start and end apart: 4 -> 0, of which waited for: 4 -> 0; matrix products, arithmetic and copies ran while one was open for 1% -> 0% of each run, Pallas kernels for 0% -> 0%
where the time goes in v3:
time: 128 us
  Pallas kernels  126 us (98%)
  local copies, waits for them, and re-layouts  1.92 us (2%)
    pallas_call x1, Pallas kernels, body(): pl.pallas_call(kernel, out_shape=jax.ShapeDtypeStruct(state.shape, state....  126 us

profile of v3, /device:TPU:1, one launch (start us, length us, event | category | flops | bytes accessed | tf_op | source)
XLA Modules:
  0.0 128.4 jit_solution(18080444714974352576)
XLA Ops:
  0.0 126.4 %triangle.1 = bf16[48,48,128]{2,1,0:T(8,128)(2,1)} custom-call(bf16[48,48,128]{2,1,0:T(8,128)(2,1)} %z_ref.1, f32[1,128]{1,0:T(1,128)} %bitcast.4, bf16[128,640]{1,0:T(8,128)(2,1)} %m1.1, f32[1,128]{1,0:T(1,128)} %bitcast.5, bf16[128,128]{1,0:T(8,128)(2,1)} %f1.1, f32[1,128]{1,0:T(1,128)} %bitcast.6, bf16[128,640]{1,0:T(8,128)(2,1)} %m2.1, ...), custom_call_target="tpu_custom_call" | custom-call | tf_op jit(solution)/shard_map/triangle/pallas_call | solution.py:532
  126.4 1.9 %copy.11 = bf16[48,48,128]{2,1,0:T(8,128)(2,1)} copy(bf16[48,48,128]{2,1,0:T(8,128)(2,1)} %triangle.1) | data formatting | bytes 1179648

commit v4 on v3

--- a/solution.py
+++ b/solution.py
@@ -55,12 +55,15 @@
     )
 
 
+def arrived(ref, sem):
+    pltpu.make_async_copy(ref, ref, sem).wait()
+
+
 BUFFERS = (
     "wt", "normed", "gate", "scale_t", "field",
     "send_b", "got_b", "send_a", "got_a",
     "row_b", "right", "row_a", "left", "send_p", "got_p", "send_o", "got_o",
-    "sb1", "rb1", "sa1", "ra1", "sb2", "rb2", "sf", "sa2", "ra2",
-    "s3", "r3", "s4", "r4", "local",
+    "sb1", "rb1", "sa1", "ra1", "sb2", "rb2", "sf", "rf", "sa2", "ra2", "s3", "r3", "s4", "r4",
 )
 
 
@@ -72,18 +75,12 @@
         vm((5 * C, C), BF16), vm((T * T, C), BF16), vm((T * T, C), F32), vm((C, C), F32),
         vm((T * T, C), BF16),
         vm(rows, BF16), vm(rows, BF16), vm(first, BF16), vm(first, BF16),
-        vm((TH, PER, 16, N), BF16), vm((2, TH, 8, 16, N), BF16),
-        vm((TH, PER, 16, N) if outgoing else (TH, PER, 2, TH, 16, 128), BF16),
+        vm((TH, PER, 16, N), BF16), vm((2, TH, 4, 2, 16, N), BF16),
+        vm((TH, PER, 16, N) if outgoing else (TH, N_ROW, TH, 16, 128), BF16),
         vm((TH, 8, 16, N) if outgoing else (TH, 2, TH, 8, 16, 128), BF16),
         vm((TH, 8, 16, N), BF16), vm((TH, PER, 16, N), BF16),
         vm(rows, BF16), vm(rows, BF16),
-        dma((TH, N_COL)), dma((TH, N_COL)), dma((TH, N_COL)), dma((TH, N_COL)),
-        dma((TH, PER)), dma((TH, N_ROW)), dma((TH, PER)),
-        dma((TH, N_ROW)), dma((TH, N_ROW)),
-        dma((TH, 8)), dma((TH, PER)),
-        dma((TH, N_COL)), dma((TH, N_COL)),
-        dma((3, TH)),
-    ]
+    ] + [dma((TH,))] * 14
 
 
 class Update:
@@ -133,52 +130,35 @@
             )
         )
 
-    def col_copy(self, sets, m, peer, slot):
-        src, dst, send, recv, _ = sets
-        return remote(
-            src.at[m, peer], dst.at[m, slot], send.at[m, peer], recv.at[m, slot], "col", peer
-        )
-
-    def col_own(self, sets, m):
-        src, dst, _, _, k = sets
-        return pltpu.make_async_copy(
-            src.at[m, self.col], dst.at[m, self.col], self.local.at[k, m]
-        )
-
     def col_start(self, sets, m):
-        each(
-            1, N_COL,
-            lambda s: self.col_copy(sets, m, lax.rem(self.col + s, N_COL), self.col).start(),
-        )
-        self.col_own(sets, m).start()
+        src, dst, send, recv = sets
+
+        def start(s):
+            peer = lax.rem(self.col + s, N_COL)
+            remote(
+                src.at[m, peer], dst.at[m, self.col], send.at[m], recv.at[m], "col", peer
+            ).start()
+
+        each(1, N_COL, start)
+        pltpu.make_async_copy(src.at[m, self.col], dst.at[m, self.col], recv.at[m]).start()
 
     def col_take(self, sets, m):
-        def landed(s):
-            peer = lax.rem(self.col + s, N_COL)
-            self.col_copy(sets, m, peer, peer).wait_recv()
-
-        each(1, N_COL, landed)
-        self.col_own(sets, m).wait()
+        arrived(sets[1].at[m], sets[3].at[m])
 
     def col_sent(self, sets, m):
-        each(
-            1, N_COL,
-            lambda s: self.col_copy(
-                sets, m, lax.rem(self.col + s, N_COL), self.col
-            ).wait_send(),
-        )
+        arrived(sets[0].at[m, 0 : N_COL - 1], sets[2].at[m])
 
     @property
     def set_b(self):
-        return self.send_b, self.got_b, self.sb1, self.rb1, 0
+        return self.send_b, self.got_b, self.sb1, self.rb1
 
     @property
     def set_a(self):
-        return self.send_a, self.got_a, self.sa1, self.ra1, 1
+        return self.send_a, self.got_a, self.sa1, self.ra1
 
     @property
     def set_o(self):
-        return self.send_o, self.got_o, self.s4, self.r4, 2
+        return self.send_o, self.got_o, self.s4, self.r4
 
     def widen_rows(self, got, out, m):
         def side(u):
@@ -218,30 +198,12 @@
         for c in range(PER):
             for u in range(2):
                 for third in range(TH):
-                    out[t, c, u, third] = self.wide[
+                    out[t, 2 * c + u, third] = self.wide[
                         u * TH + third, pl.ds(c, 16, stride=8), :
                     ].astype(BF16)
 
-    def place_b(self, m, source):
-        return self.right.at[source // 8, m, lax.rem(source, 8)]
-
-    def copy_b(self, m, c, source, peer):
-        return remote(
-            self.row_b.at[m, c], self.place_b(m, source), self.sb2.at[m, c],
-            self.rb2.at[m, source], "row", peer,
-        )
-
-    def own_b(self, m):
-        return pltpu.make_async_copy(
-            self.row_b.at[m, self.chan], self.place_b(m, self.row), self.rb2.at[m, self.row]
-        )
-
-    def hand(self, m, source):
-        there = self.place_b(m, source)
-        return remote(
-            there, there, self.sf.at[m, source // 2], self.rb2.at[m, source], "row",
-            self.chan * 2 + (1 - self.half),
-        )
+    def place_b(self, m):
+        return self.right.at[self.row // 8, m, lax.rem(self.row, 8) // 2, self.half]
 
     def spread_b(self, m):
         self.col_take(self.set_b, m)
@@ -249,59 +211,63 @@
 
         def send(s):
             c = lax.rem(self.chan + s, PER)
-            self.copy_b(m, c, self.row, 2 * c + self.half).start()
+            remote(
+                self.row_b.at[m, c], self.place_b(m), self.sb2.at[m], self.rb2.at[m],
+                "row", 2 * c + self.half,
+            ).start()
 
         each(1, PER, send)
-        self.own_b(m).start()
+        pltpu.make_async_copy(
+            self.row_b.at[m, self.chan], self.place_b(m), self.rb2.at[m]
+        ).start()
+
+    def hand(self, m):
+        there = self.right.at[:, m, :, self.half]
+        return remote(
+            there, there, self.sf.at[m], self.rf.at[m], "row", self.chan * 2 + (1 - self.half)
+        )
 
     def pass_b(self, m):
-        def pass_on(s):
-            c = lax.rem(self.chan + s, PER)
-            source = 2 * c + self.half
-            self.copy_b(m, c, source, source).wait_recv()
-            self.hand(m, source).start()
-
-        self.own_b(m).wait()
-        self.hand(m, self.row).start()
-        each(1, PER, pass_on)
+        arrived(self.right.at[:, m, :, self.half], self.rb2.at[m])
+        self.hand(m).start()
 
     def take_b(self, m):
-        each(0, PER, lambda c: self.hand(m, 2 * c + (1 - self.half)).wait_recv())
+        arrived(self.right.at[:, m, :, 1 - self.half], self.rf.at[m])
 
     def sent_b(self, m):
-        each(
-            1, PER,
-            lambda s: self.copy_b(
-                m, lax.rem(self.chan + s, PER), self.row, self.row
-            ).wait_send(),
-        )
-        each(0, PER, lambda c: self.hand(m, 2 * c + self.half).wait_send())
-
-    def pair_a(self, m, s, source):
+        arrived(self.row_b.at[m, 0 : PER - 1], self.sb2.at[m])
+        self.hand(m).wait_send()
+
+    def start_a(self, m):
         if self.outgoing:
-            return self.row_a.at[m, s], self.left.at[m, lax.rem(source, 8)], 2 * s + source // 8
-        there = self.left.at[m, source // 8, :, lax.rem(source, 8)]
-        return self.row_a.at[m, s // 2, lax.rem(s, 2)], there, s
-
-    def each_a(self, m, remote_step, own_step):
+            there = self.left.at[m, lax.rem(self.row, 8)]
+        else:
+            there = self.left.at[m, self.row // 8, :, lax.rem(self.row, 8)]
+
         def step(s):
-            src, dst, peer = self.pair_a(m, s, self.row)
+            peer = 2 * s + self.row // 8 if self.outgoing else s
+            src = self.row_a.at[m, s]
 
             @pl.when(peer != self.row)
             def _():
-                remote_step(
-                    remote(
-                        src, dst, self.sa2.at[m, s], self.ra2.at[m, self.row], "row", peer
-                    )
-                )
-
-            if own_step is not None:
-
-                @pl.when(peer == self.row)
-                def _():
-                    own_step(pltpu.make_async_copy(src, dst, self.ra2.at[m, self.row]))
+                remote(src, there, self.sa2.at[m], self.ra2.at[m], "row", peer).start()
+
+            @pl.when(peer == self.row)
+            def _():
+                pltpu.make_async_copy(src, there, self.ra2.at[m]).start()
 
         each(0, 8 if self.outgoing else 16, step)
+
+    def sent_some(self, ref, m, sem):
+        mine = self.row // 8 == self.half
+
+        @pl.when(mine)
+        def _():
+            arrived(ref.at[m, 0:7], sem.at[m])
+
+        @pl.when(jnp.logical_not(mine))
+        def _():
+            arrived(ref.at[m], sem.at[m])
 
     def spread_a(self, m):
         self.col_take(self.set_a, m)
@@ -309,39 +275,16 @@
             self.widen_rows(self.got_a, self.row_a, m)
         else:
             self.widen_lanes(self.got_a, self.row_a, m)
-        self.each_a(m, lambda copy: copy.start(), lambda copy: copy.start())
+        self.start_a(m)
 
     def take_a(self, m):
-        def step(s):
-            source = self.half * 8 + s if self.outgoing else s
-            src, dst, _ = self.pair_a(m, 0, source)
-
-            @pl.when(source != self.row)
-            def _():
-                remote(
-                    src, dst, self.sa2.at[m, 0], self.ra2.at[m, source], "row", source
-                ).wait_recv()
-
-            @pl.when(source == self.row)
-            def _():
-                pltpu.make_async_copy(src, dst, self.ra2.at[m, source]).wait()
-
-        each(0, 8 if self.outgoing else 16, step)
+        arrived(self.left.at[m], self.ra2.at[m])
 
     def sent_a(self, m):
-        self.each_a(m, lambda copy: copy.wait_send(), None)
-
-    def copy_p(self, m, s, peer, slot):
-        return remote(
-            self.send_p.at[m, s], self.got_p.at[m, slot], self.s3.at[m, s],
-            self.r3.at[m, slot], "row", peer,
-        )
-
-    def own_p(self, m):
-        return pltpu.make_async_copy(
-            self.send_p.at[m, lax.rem(self.row, 8)], self.got_p.at[m, self.chan],
-            self.r3.at[m, self.chan],
-        )
+        if self.outgoing:
+            self.sent_some(self.row_a, m, self.sa2)
+        else:
+            arrived(self.row_a.at[m, 0 : N_ROW - 1], self.sa2.at[m])
 
     def multiply(self, m):
         right = self.right[...].reshape(N, N)
@@ -358,39 +301,23 @@
         def send(s):
             peer = self.half * 8 + s
 
+            src, there = self.send_p.at[m, s], self.got_p.at[m, self.chan]
+
             @pl.when(peer != self.row)
             def _():
-                self.copy_p(m, s, peer, self.chan).start()
+                remote(src, there, self.s3.at[m], self.r3.at[m], "row", peer).start()
+
+            @pl.when(peer == self.row)
+            def _():
+                pltpu.make_async_copy(src, there, self.r3.at[m]).start()
 
         each(0, 8, send)
 
-        @pl.when(self.row // 8 == self.half)
-        def _():
-            self.own_p(m).start()
-
     def sent_p(self, m):
-        def step(s):
-            peer = self.half * 8 + s
-
-            @pl.when(peer != self.row)
-            def _():
-                self.copy_p(m, s, peer, self.chan).wait_send()
-
-        each(0, 8, step)
+        self.sent_some(self.send_p, m, self.s3)
 
     def back(self, m):
-        def take(c):
-            source = 2 * c + self.row // 8
-
-            @pl.when(source != self.row)
-            def _():
-                self.copy_p(m, 0, source, c).wait_recv()
-
-            @pl.when(source == self.row)
-            def _():
-                self.own_p(m).wait()
-
-        each(0, PER, take)
+        arrived(self.got_p.at[m], self.r3.at[m])
         for c in range(PER):
             for tile in range(2 * TH):
                 self.wide[tile, pl.ds(c, 16, stride=8), :] = self.got_p[
@@ -512,6 +439,7 @@
         two.col_start(two.set_a, m)
     each(0, IH, two.gating)
     two.middle()
+    one.sent()
     for m in range(TH):
         two.col_take(two.set_o, m)
 
@@ -524,7 +452,6 @@
                 ].reshape(8, 16, C)
 
         each(0, 2, close)
-    one.sent()
     two.sent()
 
 

time: 128 us -> 115 us (0.90)
  Pallas kernels: 126 us -> 113 us
    pallas_call x1, Pallas kernels: 126 us -> 113 us  [body(): pl.pallas_call(kernel, out_shape=jax.ShapeDtypeStruct(state.shape, state....]
where the time goes in v4:
time: 115 us
  Pallas kernels  113 us (98%)
  local copies, waits for them, and re-layouts  1.92 us (2%)
    pallas_call x1, Pallas kernels, body(): pl.pallas_call(kernel, out_shape=jax.ShapeDtypeStruct(state.shape, state....  113 us

profile of v4, /device:TPU:1, one launch (start us, length us, event | category | flops | bytes accessed | tf_op | source)
XLA Modules:
  0.0 114.5 jit_solution(8041069006707637935)
XLA Ops:
  0.0 112.6 %triangle.1 = bf16[48,48,128]{2,1,0:T(8,128)(2,1)} custom-call(bf16[48,48,128]{2,1,0:T(8,128)(2,1)} %z_ref.1, f32[1,128]{1,0:T(1,128)} %bitcast.4, bf16[128,640]{1,0:T(8,128)(2,1)} %m1.1, f32[1,128]{1,0:T(1,128)} %bitcast.5, bf16[128,128]{1,0:T(8,128)(2,1)} %f1.1, f32[1,128]{1,0:T(1,128)} %bitcast.6, bf16[128,640]{1,0:T(8,128)(2,1)} %m2.1, ...), custom_call_target="tpu_custom_call" | custom-call | tf_op jit(solution)/shard_map/triangle/pallas_call | solution.py:459
  112.6 1.9 %copy.11 = bf16[48,48,128]{2,1,0:T(8,128)(2,1)} copy(bf16[48,48,128]{2,1,0:T(8,128)(2,1)} %triangle.1) | data formatting | bytes 1179648

commit v5 on v4

--- a/solution.py
+++ b/solution.py
@@ -386,7 +386,13 @@
             self.col_sent(self.set_o, m)
 
 
-def kernel(z_ref, n1, m1, s1, f1, n2, m2, s2, f2, out_ref, wide, *refs):
+def kernel(*refs):
+    given, (out_ref, wide, loads), held, refs = refs[:9], refs[9:12], refs[12:21], refs[21:]
+    z_ref, n1, m1, s1, f1, n2, m2, s2, f2 = held
+
+    def load_of(i):
+        return pltpu.make_async_copy(given[i], held[i], loads.at[i])
+
     count = len(refs) // 2
     one = Update(True, wide, n1, m1, s1, f1, refs[:count])
     two = Update(False, wide, n2, m2, s2, f2, refs[count:])
@@ -399,6 +405,10 @@
             )
 
     each(1, 16, greet)
+    for i in (0, 2, 1, 3, 4, 5, 6, 7, 8):
+        load_of(i).start()
+    for i in (2, 3, 0, 1):
+        load_of(i).wait()
     one.ready()
     for m in range(TH):
 
@@ -420,6 +430,8 @@
         one.make_a(m)
         one.col_start(one.set_a, m)
     each(0, IH, one.gating)
+    for i in range(4, 9):
+        load_of(i).wait()
     two.ready()
     one.middle()
     for m in range(TH):
@@ -459,7 +471,19 @@
     return pl.pallas_call(
         kernel,
         out_shape=jax.ShapeDtypeStruct(state.shape, state.dtype),
-        scratch_shapes=[pltpu.VMEM((2 * TH, 16 * PER, 128), F32)]
+        in_specs=[pl.BlockSpec(memory_space=pltpu.HBM)] * 9,
+        scratch_shapes=[
+            pltpu.VMEM((2 * TH, 16 * PER, 128), F32),
+            pltpu.SemaphoreType.DMA((9,)),
+            pltpu.VMEM(state.shape, BF16),
+        ]
+        + [
+            pltpu.VMEM(shape, kind)
+            for shape, kind in (
+                ((1, C), F32), ((C, 5 * C), BF16), ((1, C), F32), ((C, C), BF16),
+            )
+        ]
+        * 2
         + buffers(True)
         + buffers(False),
         name="triangle",

time: 115 us -> 114 us (level)
  no operation moved by 1% of the time
where the time goes in v5:
time: 114 us
  Pallas kernels  112 us (98%)
  local copies, waits for them, and re-layouts  1.92 us (2%)
    pallas_call x1, Pallas kernels, body(): pl.pallas_call(kernel, out_shape=jax.ShapeDtypeStruct(state.shape, state....  112 us

profile of v5, /device:TPU:1, one launch (start us, length us, event | category | flops | bytes accessed | tf_op | source)
XLA Modules:
  0.0 113.7 jit_solution(17923964191600587909)
XLA Ops:
  0.0 111.7 %triangle.1 = bf16[48,48,128]{2,1,0:T(8,128)(2,1)} custom-call(bf16[48,48,128]{2,1,0:T(8,128)(2,1)} %refs_0_.1, f32[1,128]{1,0:T(1,128)} %bitcast.4, bf16[128,640]{1,0:T(8,128)(2,1)} %refs_2_.1, f32[1,128]{1,0:T(1,128)} %bitcast.5, bf16[128,128]{1,0:T(8,128)(2,1)} %refs_4_.1, f32[1,128]{1,0:T(1,128)} %bitcast.6, bf16[128,640]{1,0:T(8,128)(2,1)} %refs_6_.1, ...), custom_call_target="tpu_custom_call" | custom-call | tf_op jit(solution)/shard_map/triangle/pallas_call | solution.py:471
  111.8 1.9 %copy.11 = bf16[48,48,128]{2,1,0:T(8,128)(2,1)} copy(bf16[48,48,128]{2,1,0:T(8,128)(2,1)} %triangle.1) | data formatting | bytes 1179648
